TPU v7x, 32 devices: a whole 2x2x4 slice. The times are simulated.
32 devices in a mesh: row: 4 (over y, core), col: 8 (over z, x).
Axes of the slice: x: 2, y: 2, z: 4, core: 2. Of those that a mesh axis runs over, the one named last changes fastest.
Arguments:
- left: bfloat16 [128, 8192], P('col', 'row'), may hold values from -6 to 6
- right: bfloat16 [128, 8192], P('row', 'col'), may hold values from -6 to 6
- proj: bfloat16 [1024, 128], replicated, may hold values from -2 to 2
- bias: float32 [128], replicated, may hold values from -1 to 1
- pair_grad: bfloat16 [256, 256, 128], P('row', 'col'), may hold values from -0.1875 to 0.1875
Outputs:
- pair_out: bfloat16 [256, 256, 128], P('row', 'col')
- left_grad: float32 [128, 8192], P('col', 'row')
- right_grad: float32 [128, 8192], P('row', 'col')
- proj_grad: float32 [1024, 128], replicated
All inputs are finite; a program needn't handle non-finite values.
Results may differ from a plain program's by a relative error of at most 0.0056.
Values may be sent and summed in bfloat16 or wider, within the bound.
A program may use at most 128 MiB of HBM per device.

v0:
```python
import jax
import jax.numpy as jnp
from jax import lax
from jax.sharding import PartitionSpec as P

CH = 32
PAIR = 128
SEQS = 128
OUTER = 1024


def shards(left, right, proj, bias, pair_grad):
    left_all = lax.all_gather(left, "col", axis=0, tiled=True)
    right_all = lax.all_gather(right, "row", axis=0, tiled=True)
    seq_count = left_all.shape[0]
    rows_here = left_all.shape[1] // CH
    cols_here = right_all.shape[1] // CH
    left_cube = left_all.reshape(seq_count, rows_here, CH)
    right_cube = right_all.reshape(seq_count, cols_here, CH)
    square = (
        jnp.einsum("sic,sje->ijce", left_cube, right_cube, preferred_element_type=jnp.float32)
        / SEQS
    )
    outers = square.astype(jnp.bfloat16).reshape(rows_here * cols_here, OUTER)
    preact = jnp.dot(outers, proj, preferred_element_type=jnp.float32) + bias
    active = jnp.maximum(preact, 0.0)
    pair_out = (active * active).astype(jnp.bfloat16).reshape(rows_here, cols_here, PAIR)
    grad_pre = (
        pair_grad.reshape(rows_here * cols_here, PAIR).astype(jnp.float32) * 2.0 * active
    ).astype(jnp.bfloat16)
    weight_term = lax.dot_general(
        outers, grad_pre, (((0,), (0,)), ((), ())), preferred_element_type=jnp.float32
    )
    proj_grad = lax.psum(weight_term, ("row", "col"))
    grad_outer = jnp.dot(grad_pre, proj.T, preferred_element_type=jnp.float32).astype(jnp.bfloat16)
    grad_cube = grad_outer.reshape(rows_here, cols_here, CH, CH)
    left_whole = (
        jnp.einsum("ijce,sje->sic", grad_cube, right_cube, preferred_element_type=jnp.float32)
        / SEQS
    )
    right_whole = (
        jnp.einsum("ijce,sic->sje", grad_cube, left_cube, preferred_element_type=jnp.float32) / SEQS
    )
    left_grad = lax.psum_scatter(
        left_whole.reshape(seq_count, rows_here * CH), "col", scatter_dimension=0, tiled=True
    )
    right_grad = lax.psum_scatter(
        right_whole.reshape(seq_count, cols_here * CH), "row", scatter_dimension=0, tiled=True
    )
    return (pair_out, left_grad, right_grad, proj_grad)


def solution(mesh):
    return jax.shard_map(
        shards,
        mesh=mesh,
        in_specs=(P("col", "row"), P("row", "col"), P(), P(), P("row", "col", None)),
        out_specs=(P("row", "col", None), P("col", "row"), P("row", "col"), P()),
        check_vma=False,
    )
```

profile of v0, /device:TPU:0, one launch (start us, length us, event | category | flops | bytes accessed | tf_op | source)
XLA Modules:
  0.0 248.4 jit_solution(3948851120335303654)
XLA Ops:
  8.0 0.0 copy-start
  8.0 0.0 all-reduce.2.cloned.1.call-start
  8.1 33.4 %all_gather.7 = bf16[128,2048]{1,0:T(8,128)(2,1)S(1)} all-gather(bf16[16,2048]{1,0:T(8,128)(2,1)} %param.5), channel_id=1, replica_groups=mesh['row'=4,'col'=8] {'col'}, dimensions={0}, use_global_device_ids=true | all-gather | bytes 589824 | tf_op jit(solution)/shard_map/all_gather | solution.py:13
  41.4 0.3 copy.26
  41.7 6.0 %all_gather.6 = bf16[128,1024]{1,0:T(8,128)(2,1)S(1)} all-gather(bf16[32,1024]{1,0:T(8,128)(2,1)} %param.6), channel_id=1, replica_groups=mesh['row'=4,'col'=8] {'row'}, dimensions={0}, use_global_device_ids=true | all-gather | bytes 327680 | tf_op jit(solution)/shard_map/all_gather | solution.py:14
  47.7 0.2 copy.25
  47.9 5.6 %fusion = bf16[64,32,32,32]{0,3,2,1:T(8,128)(2,1)} fusion(bf16[128,32,32,1]{0,2,3,1:T(8,128)(2,1)S(1)} %bitcast.50, bf16[128,64,32]{0,2,1:T(8,128)(2,1)S(1)} %bitcast.48), kind=kOutput, calls=%fused_computation.1 | convolution fusion | flops 541065216 | bytes 4980736 | tf_op jit(solution)/shard_map/sic,sje->ijce/dot_general | solution.py:21
  53.5 24.6 %copy.28 = bf16[64,32,32,32]{3,2,1,0:T(8,128)(2,1)} copy(bf16[64,32,32,32]{0,3,2,1:T(8,128)(2,1)} %fusion) | data formatting | bytes 8388608 | tf_op jit(solution)/shard_map/convert_element_type | solution.py:24
  78.1 0.0 copy-start.2
  78.1 0.0 copy-start.3
  78.1 23.3 %reshape.36 = bf16[2048,1024]{1,0:T(8,128)(2,1)} reshape(bf16[64,32,32,32]{3,2,1,0:T(8,128)(2,1)} %copy.28) | data formatting | bytes 8388608 | tf_op jit(solution)/shard_map/reshape | solution.py:24
  101.4 0.0 copy-done.2
  101.4 0.0 copy-start.1
  101.4 0.1 convert_multiply_fusion
  101.6 0.0 copy-done
  101.6 0.0 copy-done.3
  101.6 4.4 %fusion.4 = (bf16[2048,128]{1,0:T(8,128)(2,1)S(1)}, bf16[2048,128]{1,0:T(8,128)(2,1)}) fusion(f32[64,32,128]{2,1,0:T(8,128)S(1)} %convert_multiply_fusion, f32[128]{0:T(128)S(1)} %copy-done.3, bf16[2048,1024]{1,0:T(8,128)(2,1)} %reshape.36, bf16[1024,128]{1,0:T(8,128)(2,1)S(1)} %copy-done), kind=kOutput, calls=%fused_computation.10 | convolution fusion | flops 538443776 | bytes 6554112 | tf_op jit(solution)/shard_map/dot_general | solution.py:25
  106.0 0.0 copy-done.1
  106.0 2.1 fusion.7
  108.1 0.0 all-reduce.2.cloned.1.call-update
  108.1 0.2 reduce-scatter.5.cloned.1.call-start
  108.3 3.2 %convolution_convert_fusion = bf16[2048,1024]{1,0:T(8,128)(2,1)} fusion(bf16[2048,128]{1,0:T(8,128)(2,1)S(1)} %get-tuple-element.4, bf16[1024,128]{1,0:T(8,128)(2,1)S(1)} %copy-done), kind=kOutput, calls=%fused_computation.2 | convolution fusion | flops 538968064 | bytes 4980736 | tf_op jit(solution)/shard_map/dot_general | solution.py:35
  111.5 20.3 %reshape.38 = bf16[64,32,32,32]{3,2,1,0:T(8,128)(2,1)} reshape(bf16[2048,1024]{1,0:T(8,128)(2,1)} %convolution_convert_fusion) | data formatting | bytes 8388608 | tf_op jit(solution)/shard_map/reshape | solution.py:36
  131.9 10.3 %fusion.3 = f32[32,32,128]{2,1,0:T(8,128)S(1)} fusion(bf16[64,32,32,32]{3,2,1,0:T(8,128)(2,1)} %reshape.38, bf16[128,64,32,1]{0,2,3,1:T(8,128)(2,1)S(1)} %bitcast.49), kind=kOutput, calls=%fused_computation.8 | convolution fusion | flops 537001984 | bytes 5242880 | tf_op jit(solution)/shard_map/ijce,sic->sje/dot_general | solution.py:42
  142.2 1.0 copy.31
  143.2 0.0 reduce-scatter.5.cloned.1.call-update
  143.2 0.0 reduce-scatter.3.cloned.1.call-start
  143.3 9.1 %fusion.2 = f32[64,32,128]{2,1,0:T(8,128)S(1)} fusion(bf16[64,32,32,32]{3,2,1,0:T(8,128)(2,1)} %reshape.38, bf16[128,32,32,1]{0,2,1,3:T(8,128)(2,1)S(1)} %bitcast.51), kind=kOutput, calls=%fused_computation.6 | convolution fusion | flops 537133056 | bytes 5505024 | tf_op jit(solution)/shard_map/ijce,sje->sic/dot_general | solution.py:38
  152.4 1.3 copy.29
  153.7 0.0 reduce-scatter.3.cloned.1.call-update
  153.8 85.4 %all-reduce.2.cloned.1.call-done = f32[1024,128]{1,0:T(8,128)} async-done(((f32[1024,128]{1,0:T(8,128)}), f32[1024,128]{1,0:T(8,128)}) %all-reduce.2.cloned.1.call-update) | async-done | bytes 524304 | tf_op jit(solution)/shard_map/psum | solution.py:34
  239.1 1.9 copy.41
  (2 shorter events, 0.0 us)
Async XLA Ops:
  8.0 93.6 %copy-start = (bf16[1024,128]{1,0:T(8,128)(2,1)S(1)}, bf16[1024,128]{1,0:T(8,128)(2,1)}, u32[]{:S(2)}) copy-start(bf16[1024,128]{1,0:T(8,128)(2,1)} %param.7) | copy-start | bytes 786436
  8.0 231.1 %all-reduce.2.cloned.1.call-start = ((), (), s32[]{:S(2)}) async-start(), calls=%async_computation.4 | async-start | bytes 1048576 | tf_op jit(solution)/shard_map/psum | solution.py:34
  78.1 23.3 %copy-start.2 = (bf16[64,32,128]{2,1,0:T(8,128)(2,1)S(1)}, bf16[64,32,128]{2,1,0:T(8,128)(2,1)}, u32[]{:S(2)}) copy-start(bf16[64,32,128]{2,1,0:T(8,128)(2,1)} %param.9) | copy-start | bytes 1572868
  78.1 23.5 %copy-start.3 = (f32[128]{0:T(128)S(1)}, f32[128]{0:T(128)}, u32[]{:S(2)}) copy-start(f32[128]{0:T(128)} %param.8) | copy-start | bytes 1540
  101.4 4.5 %copy-start.1 = (bf16[2048,1024]{1,0:T(8,128)(2,1)S(1)}, bf16[2048,1024]{1,0:T(8,128)(2,1)}, u32[]{:S(2)}) copy-start(bf16[2048,1024]{1,0:T(8,128)(2,1)} %reshape.36) | copy-start | bytes 12582916
  108.1 131.0 %reduce-scatter.5.cloned.1.call-start = ((), (), s32[]{:S(2)}) async-start(), calls=%async_computation.3 | async-start | bytes 655360 | tf_op jit(solution)/shard_map/reduce_scatter | solution.py:47
  143.2 95.9 %reduce-scatter.3.cloned.1.call-start = ((), (), s32[]{:S(2)}) async-start(), calls=%async_computation.2 | async-start | bytes 1179648 | tf_op jit(solution)/shard_map/reduce_scatter | solution.py:44
Sparse Core Ops, SparseCore 0:
  108.2 130.8 all-reduce.1
Sparse Core Ops, SparseCore 1:
  143.3 22.7 reduce-scatter.4
  169.9 64.3 reduce-scatter.2
where the time goes:
time: 250 us; the launch traced here: 248 us
  waiting for transfers between devices  85.4 us (34%)
  local copies, waits for them, and re-layouts  72.9 us (29%)
  blocking collectives  39.4 us (16%)
  matrix products  34.8 us (14%)
  between operations  15.5 us (6%)
    psum x1, waiting for transfers between devices, shards(): proj_grad = lax.psum(weight_term, ('row', 'col'))  85.4 us
    all_gather x1, blocking collectives, shards(): left_all = lax.all_gather(left, 'col', axis=0, tiled=True)  33.4 us
    convert_element_type x1, local copies, waits for them, and re-layouts, shards(): outers = square.astype(jnp.bfloat16).reshape(rows_here * cols_here, OUTER)  24.6 us
    reshape x1, local copies, waits for them, and re-layouts, shards(): outers = square.astype(jnp.bfloat16).reshape(rows_here * cols_here, OUTER)  23.3 us
    reshape x1, local copies, waits for them, and re-layouts, shards(): grad_cube = grad_outer.reshape(rows_here, cols_here, CH, CH)  20.3 us
    dot_general x1, matrix products, shards(): jnp.einsum('ijce,sic->sje', grad_cube, left_cube, preferred_element_type=...  10.3 us
    dot_general x1, matrix products, shards(): jnp.einsum('ijce,sje->sic', grad_cube, right_cube, preferred_element_type...  9.14 us
    all_gather x1, blocking collectives, shards(): right_all = lax.all_gather(right, 'row', axis=0, tiled=True)  5.99 us
  transfers between devices with their start and end apart: 3, of which 1 were waited for; matrix products, arithmetic and copies ran while one was open for 18% of the time, Pallas kernels for 0%

commit v1 on v0

--- a/solution.py
+++ b/solution.py
@@ -31,7 +31,10 @@
     weight_term = lax.dot_general(
         outers, grad_pre, (((0,), (0,)), ((), ())), preferred_element_type=jnp.float32
     )
-    proj_grad = lax.psum(weight_term, ("row", "col"))
+    list_cells = lambda t0, bus_axis, axis_tag: lax.psum(
+        lax.psum(t0, axis_name=bus_axis), axis_name=axis_tag
+    )
+    proj_grad = list_cells(weight_term, bus_axis="col", axis_tag="row")
     grad_outer = jnp.dot(grad_pre, proj.T, preferred_element_type=jnp.float32).astype(jnp.bfloat16)
     grad_cube = grad_outer.reshape(rows_here, cols_here, CH, CH)
     left_whole = (

time: 250 us -> 319 us (1.28)
  waiting for transfers between devices: 85.4 us -> 156 us
    reduce_scatter x1, waiting for transfers between devices: 0.01 us -> 68 us  [shards(): lax.psum_scatter(left_whole.reshape(seq_count, rows_here * CH), 'col', sc...]
    reduce_scatter x1, waiting for transfers between devices: 0.01 us -> 24.8 us  [shards(): lax.psum_scatter(right_whole.reshape(seq_count, cols_here * CH), 'row', s...]
    psum x1 -> x2, waiting for transfers between devices: 85.4 us -> 63.2 us  [the longest x1 50.4 us: shards(): lax.psum(t0, axis_name=bus_axis)]
  transfers between devices with their start and end apart: 3 -> 4, of which waited for: 1 -> 4; matrix products, arithmetic and copies ran while one was open for 18% -> 14% of each run, Pallas kernels for 0% -> 0%
where the time goes in v1:
time: 319 us; the launch traced here: 317 us
  waiting for transfers between devices  156 us (49%)
  local copies, waits for them, and re-layouts  72.9 us (23%)
  blocking collectives  39.4 us (12%)
  matrix products  34.8 us (11%)
  between operations  13.8 us (4%)
    reduce_scatter x1, waiting for transfers between devices, shards(): lax.psum_scatter(left_whole.reshape(seq_count, rows_here * CH), 'col', sc...  68 us
    psum x1, waiting for transfers between devices, shards(): lax.psum(t0, axis_name=bus_axis)  50.4 us
    all_gather x1, blocking collectives, shards(): left_all = lax.all_gather(left, 'col', axis=0, tiled=True)  33.4 us
    reduce_scatter x1, waiting for transfers between devices, shards(): lax.psum_scatter(right_whole.reshape(seq_count, cols_here * CH), 'row', s...  24.8 us
    convert_element_type x1, local copies, waits for them, and re-layouts, shards(): outers = square.astype(jnp.bfloat16).reshape(rows_here * cols_here, OUTER)  24.6 us
    reshape x1, local copies, waits for them, and re-layouts, shards(): outers = square.astype(jnp.bfloat16).reshape(rows_here * cols_here, OUTER)  23.3 us
    reshape x1, local copies, waits for them, and re-layouts, shards(): grad_cube = grad_outer.reshape(rows_here, cols_here, CH, CH)  20.3 us
    psum x1, waiting for transfers between devices, shards(): lax.psum(lax.psum(t0, axis_name=bus_axis), axis_name=axis_tag)  12.8 us
  transfers between devices with their start and end apart: 4, of which 4 were waited for; matrix products, arithmetic and copies ran while one was open for 14% of the time, Pallas kernels for 0%

profile of v1, /device:TPU:0, one launch (start us, length us, event | category | flops | bytes accessed | tf_op | source)
XLA Modules:
  0.0 317.3 jit_solution(17756645603200646269)
XLA Ops:
  7.2 0.0 copy-start
  7.2 0.0 all-reduce.3.cloned.1.call-start
  7.2 33.4 %all_gather.7 = bf16[128,2048]{1,0:T(8,128)(2,1)S(1)} all-gather(bf16[16,2048]{1,0:T(8,128)(2,1)} %param.5), channel_id=1, replica_groups=mesh['row'=4,'col'=8] {'col'}, dimensions={0}, use_global_device_ids=true | all-gather | bytes 589824 | tf_op jit(solution)/shard_map/all_gather | solution.py:13
  40.6 0.3 copy.26
  40.9 6.0 %all_gather.6 = bf16[128,1024]{1,0:T(8,128)(2,1)S(1)} all-gather(bf16[32,1024]{1,0:T(8,128)(2,1)} %param.6), channel_id=1, replica_groups=mesh['row'=4,'col'=8] {'row'}, dimensions={0}, use_global_device_ids=true | all-gather | bytes 327680 | tf_op jit(solution)/shard_map/all_gather | solution.py:14
  46.9 0.2 copy.25
  47.1 5.6 %fusion = bf16[64,32,32,32]{0,3,2,1:T(8,128)(2,1)} fusion(bf16[128,32,32,1]{0,2,3,1:T(8,128)(2,1)S(1)} %bitcast.50, bf16[128,64,32]{0,2,1:T(8,128)(2,1)S(1)} %bitcast.48), kind=kOutput, calls=%fused_computation.1 | convolution fusion | flops 541065216 | bytes 4980736 | tf_op jit(solution)/shard_map/sic,sje->ijce/dot_general | solution.py:21
  52.7 24.6 %copy.28 = bf16[64,32,32,32]{3,2,1,0:T(8,128)(2,1)} copy(bf16[64,32,32,32]{0,3,2,1:T(8,128)(2,1)} %fusion) | data formatting | bytes 8388608 | tf_op jit(solution)/shard_map/convert_element_type | solution.py:24
  77.3 23.3 %reshape.36 = bf16[2048,1024]{1,0:T(8,128)(2,1)} reshape(bf16[64,32,32,32]{3,2,1,0:T(8,128)(2,1)} %copy.28) | data formatting | bytes 8388608 | tf_op jit(solution)/shard_map/reshape | solution.py:24
  100.6 0.0 copy-done.2
  100.6 0.1 convert_multiply_fusion
  100.7 4.4 %fusion.4 = (bf16[2048,128]{1,0:T(8,128)(2,1)S(1)}, bf16[2048,128]{1,0:T(8,128)(2,1)}) fusion(f32[64,32,128]{2,1,0:T(8,128)S(1)} %convert_multiply_fusion, f32[128]{0:T(128)S(1)} %copy-done.3, bf16[2048,1024]{1,0:T(8,128)(2,1)} %reshape.36, bf16[1024,128]{1,0:T(8,128)(2,1)S(1)} %copy-done), kind=kOutput, calls=%fused_computation.10 | convolution fusion | flops 538443776 | bytes 6554112 | tf_op jit(solution)/shard_map/dot_general | solution.py:25
  105.1 0.0 copy-done.1
  105.1 2.1 fusion.7
  107.2 0.0 all-reduce.3.cloned.1.call-update
  107.3 0.0 all-reduce.5.cloned.1.call-start
  107.3 3.2 %convolution_convert_fusion = bf16[2048,1024]{1,0:T(8,128)(2,1)} fusion(bf16[2048,128]{1,0:T(8,128)(2,1)S(1)} %get-tuple-element.4, bf16[1024,128]{1,0:T(8,128)(2,1)S(1)} %copy-done), kind=kOutput, calls=%fused_computation.2 | convolution fusion | flops 538968064 | bytes 4980736 | tf_op jit(solution)/shard_map/dot_general | solution.py:38
  110.5 20.3 %reshape.38 = bf16[64,32,32,32]{3,2,1,0:T(8,128)(2,1)} reshape(bf16[2048,1024]{1,0:T(8,128)(2,1)} %convolution_convert_fusion) | data formatting | bytes 8388608 | tf_op jit(solution)/shard_map/reshape | solution.py:39
  130.8 50.4 %all-reduce.3.cloned.1.call-done = f32[1024,128]{1,0:T(8,128)} async-done(((f32[1024,128]{1,0:T(8,128)}), f32[1024,128]{1,0:T(8,128)}) %all-reduce.3.cloned.1.call-update) | async-done | bytes 524304 | tf_op jit(solution)/shard_map/psum | solution.py:35
  181.2 0.0 all-reduce.5.cloned.1.call-update
  181.2 0.2 reduce-scatter.5.cloned.1.call-start
  181.4 10.3 %fusion.3 = f32[32,32,128]{2,1,0:T(8,128)S(1)} fusion(bf16[64,32,32,32]{3,2,1,0:T(8,128)(2,1)} %reshape.38, bf16[128,64,32,1]{0,2,3,1:T(8,128)(2,1)S(1)} %bitcast.49), kind=kOutput, calls=%fused_computation.8 | convolution fusion | flops 537001984 | bytes 5242880 | tf_op jit(solution)/shard_map/ijce,sic->sje/dot_general | solution.py:45
  191.7 1.0 copy.31
  192.7 0.0 reduce-scatter.5.cloned.1.call-update
  192.7 0.0 reduce-scatter.3.cloned.1.call-start
  192.8 9.2 %fusion.2 = f32[64,32,128]{2,1,0:T(8,128)S(1)} fusion(bf16[64,32,32,32]{3,2,1,0:T(8,128)(2,1)} %reshape.38, bf16[128,32,32,1]{0,2,1,3:T(8,128)(2,1)S(1)} %bitcast.51), kind=kOutput, calls=%fused_computation.6 | convolution fusion | flops 537133056 | bytes 5505024 | tf_op jit(solution)/shard_map/ijce,sje->sic/dot_general | solution.py:41
  202.0 1.3 copy.29
  203.3 0.0 reduce-scatter.3.cloned.1.call-update
  203.3 12.8 %all-reduce.5.cloned.1.call-done = f32[1024,128]{1,0:T(8,128)} async-done(((f32[1024,128]{1,0:T(8,128)}), f32[1024,128]{1,0:T(8,128)}) %all-reduce.5.cloned.1.call-update) | async-done | bytes 524304 | tf_op jit(solution)/shard_map/psum | solution.py:34
  216.1 24.8 %reduce-scatter.5.cloned.1.call-done = f32[32,1024]{1,0:T(8,128)} async-done(((f32[128,1024]{1,0:T(8,128)}), f32[32,1024]{1,0:T(8,128)}) %reduce-scatter.5.cloned.1.call-update) | async-done | bytes 131088 | tf_op jit(solution)/shard_map/reduce_scatter | solution.py:50
  241.0 68.0 %reduce-scatter.3.cloned.1.call-done = f32[16,2048]{1,0:T(8,128)} async-done(((f32[128,2048]{1,0:T(8,128)}), f32[16,2048]{1,0:T(8,128)}) %reduce-scatter.3.cloned.1.call-update) | async-done | bytes 131088 | tf_op jit(solution)/shard_map/reduce_scatter | solution.py:47
  308.9 1.9 copy.42
  (5 shorter events, 0.0 us)
Async XLA Ops:
  7.2 93.6 %copy-start = (bf16[1024,128]{1,0:T(8,128)(2,1)S(1)}, bf16[1024,128]{1,0:T(8,128)(2,1)}, u32[]{:S(2)}) copy-start(bf16[1024,128]{1,0:T(8,128)(2,1)} %param.7) | copy-start | bytes 786436
  7.2 174.0 %all-reduce.3.cloned.1.call-start = ((), (), s32[]{:S(2)}) async-start(), calls=%async_computation.4 | async-start | bytes 1048576 | tf_op jit(solution)/shard_map/psum | solution.py:35
  77.3 23.3 %copy-start.2 = (bf16[64,32,128]{2,1,0:T(8,128)(2,1)S(1)}, bf16[64,32,128]{2,1,0:T(8,128)(2,1)}, u32[]{:S(2)}) copy-start(bf16[64,32,128]{2,1,0:T(8,128)(2,1)} %param.9) | copy-start | bytes 1572868
  77.3 23.5 %copy-start.3 = (f32[128]{0:T(128)S(1)}, f32[128]{0:T(128)}, u32[]{:S(2)}) copy-start(f32[128]{0:T(128)} %param.8) | copy-start | bytes 1540
  100.6 4.5 %copy-start.1 = (bf16[2048,1024]{1,0:T(8,128)(2,1)S(1)}, bf16[2048,1024]{1,0:T(8,128)(2,1)}, u32[]{:S(2)}) copy-start(bf16[2048,1024]{1,0:T(8,128)(2,1)} %reshape.36) | copy-start | bytes 12582916
  107.3 108.9 %all-reduce.5.cloned.1.call-start = ((), (), s32[]{:S(2)}) async-start(), calls=%async_computation.5 | async-start | bytes 1048576 | tf_op jit(solution)/shard_map/psum | solution.py:34
  181.2 59.8 %reduce-scatter.5.cloned.1.call-start = ((), (), s32[]{:S(2)}) async-start(), calls=%async_computation.3 | async-start | bytes 655360 | tf_op jit(solution)/shard_map/reduce_scatter | solution.py:50
  192.7 116.2 %reduce-scatter.3.cloned.1.call-start = ((), (), s32[]{:S(2)}) async-start(), calls=%async_computation.2 | async-start | bytes 1179648 | tf_op jit(solution)/shard_map/reduce_scatter | solution.py:47
Sparse Core Ops, SparseCore 0:
  107.4 73.7 all-reduce.2
  183.5 32.5 all-reduce.4
  219.2 21.7 reduce-scatter.4
  244.8 64.0 reduce-scatter.2
